TPU v7x, 32 devices: a whole 2x2x4 slice. The times are simulated.
32 devices in a mesh: dp: 16 (over z, y, x), mp: 2 (over core).
Axes of the slice: x: 2, y: 2, z: 4, core: 2. Of those that a mesh axis runs over, the one named last changes fastest.
Arguments:
- new_embed: bfloat16 [1792, 1280], P('dp'), may hold values from -3 to 3
- context_key_cache: bfloat16 [1792, 16, 1280], P('dp', None, 'mp'), may hold values from -2500 to 2500
- value_cache: bfloat16 [1792, 16, 1280], P('dp', None, 'mp'), may hold values from -6 to 6
- valid: int32 [1792], P('dp'), may hold values from 2 to 16
- attn_gain: float32 [1280], replicated, may hold values from 0.1 to 1.9
- mlp_gain: float32 [1280], replicated, may hold values from 0.1 to 1.9
- query_scale: float32 [80], replicated, may hold values from 0.1 to 1.9
- w_qkv: bfloat16 [3, 1280, 1280], P(None, 'dp', 'mp'), may hold values from -0.15625 to 0.15625
- w_out: bfloat16 [1280, 1280], P('mp', 'dp'), may hold values from -0.625 to 0.625
- w_up: bfloat16 [1280, 1280], P('dp', 'mp'), may hold values from -0.15625 to 0.15625
- w_down: bfloat16 [1280, 1280], P('mp', 'dp'), may hold values from -0.15625 to 0.15625
- head_hidden: bfloat16 [1280, 1280], P('dp', 'mp'), may hold values from -0.15625 to 0.15625
- final_layer_matrices: bfloat16 [2, 1280, 1280], P(None, 'mp', 'dp'), may hold values from -0.15625 to 0.15625
Outputs:
- predicted_levels: float32 [1792, 1280], P('dp', 'mp')
Inputs may be any that keep to these rules, and one draw needn't show every extreme that they name: Series s uses its first valid[s] cached patches.
All inputs are finite; a program needn't handle non-finite values.
Results may differ from a plain program's by a relative error of at most 0.035.
Values may be sent and summed in bfloat16 or wider, within the bound.
A program may use at most 128 MiB of HBM per device.

v0:
```python
import math

import jax
import jax.numpy as jnp
from jax import lax
from jax.sharding import PartitionSpec as P

D = 1280
HEADS = 16


def rms_scale(values, gain):
    meansq = jnp.mean(values * values, axis=-1, keepdims=True)
    return values * lax.rsqrt(meansq + 1e-06) * gain


def per_device(
    new_embed,
    context_key_cache,
    value_cache,
    valid,
    attn_gain,
    mlp_gain,
    query_scale,
    w_qkv,
    w_out,
    w_up,
    w_down,
    head_hidden,
    final_layer_matrices,
):
    row_count = new_embed.shape[0]
    context_len = context_key_cache.shape[1]
    local_width = context_key_cache.shape[2]
    single_lane_dimension = D // HEADS
    local_heads = local_width // single_lane_dimension
    mp_index = lax.axis_index("mp")
    stream = new_embed.astype(jnp.float32)
    normed = rms_scale(stream, attn_gain).astype(jnp.bfloat16)
    combined_attend_triple = lax.all_gather(w_qkv, "dp", axis=1, tiled=True)
    projected = jnp.einsum(
        "sd,jde->jse", normed, combined_attend_triple, preferred_element_type=jnp.float32
    )
    query_all = projected[0].reshape(row_count, local_heads, single_lane_dimension)
    query_all = (query_all * query_scale / math.sqrt(single_lane_dimension)).astype(jnp.bfloat16)
    key_new = (
        projected[1].astype(jnp.bfloat16).reshape(row_count, local_heads, single_lane_dimension)
    )
    value_new = (
        projected[2].astype(jnp.bfloat16).reshape(row_count, local_heads, single_lane_dimension)
    )
    cache_keys = context_key_cache.reshape(
        row_count, context_len, local_heads, single_lane_dimension
    )
    cache_vals = value_cache.reshape(row_count, context_len, local_heads, single_lane_dimension)
    scores = jnp.einsum("bhe,bche->bhc", query_all, cache_keys, preferred_element_type=jnp.float32)
    own_score = jnp.sum(query_all.astype(jnp.float32) * key_new.astype(jnp.float32), axis=-1)
    in_use = jnp.arange(context_len, dtype=jnp.int32)[None, :] < valid[:, None]
    scores = jnp.where(in_use[:, None, :], scores, -jnp.inf)
    highest = jnp.maximum(jnp.max(scores, axis=-1), own_score)
    exp_cache = jnp.exp(scores - highest[..., None])
    exp_own = jnp.exp(own_score - highest)
    denominator = jnp.sum(exp_cache, axis=-1) + exp_own
    weight_cache = (exp_cache / denominator[..., None]).astype(jnp.bfloat16)
    weight_own = (exp_own / denominator).astype(jnp.bfloat16)
    context = jnp.einsum(
        "bhc,bche->bhe", weight_cache, cache_vals, preferred_element_type=jnp.float32
    )
    context = context + weight_own.astype(jnp.float32)[..., None] * value_new.astype(jnp.float32)
    context = context.astype(jnp.bfloat16).reshape(row_count, local_width)
    attention = jnp.dot(
        context, lax.all_gather(w_out, "dp", axis=1, tiled=True), preferred_element_type=jnp.float32
    )
    stream1 = stream + lax.psum(attention.astype(jnp.bfloat16), "mp").astype(jnp.float32)
    normed2 = rms_scale(stream1, mlp_gain).astype(jnp.bfloat16)
    up_projection_full = lax.all_gather(w_up, "dp", axis=0, tiled=True)
    up_act = jnp.dot(normed2, up_projection_full, preferred_element_type=jnp.float32)
    hidden = jax.nn.relu(up_act).astype(jnp.bfloat16)
    feed_out = jnp.dot(
        hidden, lax.all_gather(w_down, "dp", axis=1, tiled=True), preferred_element_type=jnp.float32
    )
    halved_width = final_layer_matrices.shape[1]
    feed_share = lax.psum_scatter(
        feed_out.astype(jnp.bfloat16), "mp", scatter_dimension=1, tiled=True
    ).astype(jnp.float32)
    stream1_half = lax.dynamic_slice_in_dim(stream1, mp_index * halved_width, halved_width, 1)
    stream_half = (stream1_half + feed_share).astype(jnp.bfloat16)
    carried_signal_second = lax.all_gather(stream_half, "mp", axis=1, tiled=True)
    hidden_full = lax.all_gather(head_hidden, "dp", axis=0, tiled=True)
    head_pre = jnp.dot(carried_signal_second, hidden_full, preferred_element_type=jnp.float32)
    quantile_layer_nonlinear = jax.nn.silu(head_pre).astype(jnp.bfloat16)
    shard_piece = lax.all_gather(final_layer_matrices, "dp", axis=2, tiled=True)
    result = jnp.dot(quantile_layer_nonlinear, shard_piece[0], preferred_element_type=jnp.float32)
    partial_out = result + jnp.dot(stream_half, shard_piece[1], preferred_element_type=jnp.float32)
    return lax.psum_scatter(
        partial_out.astype(jnp.bfloat16), "mp", scatter_dimension=1, tiled=True
    ).astype(jnp.float32)


def solution(mesh):
    in_specs = (
        P("dp", None),
        P("dp", None, "mp"),
        P("dp", None, "mp"),
        P("dp"),
        P(),
        P(),
        P(),
        P(None, "dp", "mp"),
        P("mp", "dp"),
        P("dp", "mp"),
        P("mp", "dp"),
        P("dp", "mp"),
        P(None, "mp", "dp"),
    )
    out_specs = P("dp", "mp")
    return jax.shard_map(
        per_device, mesh=mesh, in_specs=in_specs, out_specs=out_specs, check_vma=False
    )
```

profile of v0, /device:TPU:13, one launch (start us, length us, event | category | flops | bytes accessed | tf_op | source)
XLA Modules:
  0.0 458.2 jit_solution(9463699573649009506)
XLA Ops:
  6.5 0.7 all-gather.7.cloned.1.call-update
  7.3 0.0 all-gather.9.cloned.1.call-start
  7.3 0.7 all-gather.9.cloned.1.call-update
  8.0 0.0 all-reduce.2.cloned.1.call-start
  8.1 4.7 %copy.46 = bf16[112,16,640]{0,2,1:T(8,128)(2,1)} copy(bf16[112,16,640]{2,1,0:T(8,128)(2,1)} %param.14) | data formatting | bytes 4587520
  12.7 3.9 copy.47
  16.6 0.1 fusion.3
  16.8 74.4 %all-gather.7.cloned.1.call-done = bf16[3,1280,640]{2,1,0:T(8,128)(2,1)} async-done(((bf16[3,80,640]{2,1,0:T(8,128)(2,1)}), bf16[3,1280,640]{2,1,0:T(8,128)(2,1)}) %all-gather.7.cloned.1.call-update) | async-done | bytes 4915216 | tf_op jit(solution)/shard_map/all_gather | solution.py:40
  91.1 4.3 fusion.25
  95.4 0.7 slice_convert_fusion
  96.2 0.2 copy.30
  96.3 1.0 slice.22
  97.3 0.9 copy.28
  98.2 1.1 multiply_reduce_fusion.3
  99.3 2.7 multiply_reduce_fusion.1
  102.1 0.7 copy.53
  102.8 0.2 copy.32
  103.0 1.7 multiply_reduce_fusion
  104.7 45.9 %all-gather.9.cloned.1.call-done = bf16[640,1280]{0,1:T(8,128)(2,1)} async-done(((bf16[640,80]{0,1:T(8,128)(2,1)}), bf16[640,1280]{0,1:T(8,128)(2,1)}) %all-gather.9.cloned.1.call-update) | async-done | bytes 1638416 | tf_op jit(solution)/shard_map/all_gather | solution.py:72
  150.6 2.8 convolution_convert_fusion.1
  153.4 0.0 all-gather.11.cloned.1.call-start
  153.4 0.5 all-gather.11.cloned.1.call-update
  153.9 0.0 all-gather.13.cloned.1.call-start
  154.0 0.5 all-gather.13.cloned.1.call-update
  154.5 0.0 reduce-scatter.7.cloned.1.call-start
  154.6 18.3 %all-reduce.2.cloned.1.call-done = bf16[112,1280]{1,0:T(8,128)(2,1)} async-done(((bf16[112,1280]{1,0:T(8,128)(2,1)}), bf16[112,1280]{1,0:T(8,128)(2,1)}) %all-reduce.2.cloned.1.call-update) | async-done | bytes 286736 | tf_op jit(solution)/shard_map/psum | solution.py:74
  172.9 1.1 convert_add_fusion
  174.1 58.5 %all-gather.11.cloned.1.call-done = bf16[1280,640]{1,0:T(8,128)(2,1)} async-done(((bf16[80,640]{1,0:T(8,128)(2,1)}), bf16[1280,640]{1,0:T(8,128)(2,1)}) %all-gather.11.cloned.1.call-update) | async-done | bytes 1638416 | tf_op jit(solution)/shard_map/all_gather | solution.py:76
  232.6 59.5 %all-gather.13.cloned.1.call-done = bf16[640,1280]{0,1:T(8,128)(2,1)} async-done(((bf16[640,80]{0,1:T(8,128)(2,1)}), bf16[640,1280]{0,1:T(8,128)(2,1)}) %all-gather.13.cloned.1.call-update) | async-done | bytes 1638416 | tf_op jit(solution)/shard_map/all_gather | solution.py:80
  292.1 3.0 convolution_convert_fusion
  295.1 0.9 copy.48
  296.0 0.0 reduce-scatter.7.cloned.1.call-update
  296.0 0.0 all-gather.15.cloned.1.call-start
  296.0 0.7 all-gather.15.cloned.1.call-update
  296.8 0.0 all-gather.17.cloned.1.call-start
  296.8 0.7 all-gather.17.cloned.1.call-update
  297.5 0.0 reduce-scatter.9.cloned.1.call-start
  297.6 7.5 %reduce-scatter.7.cloned.1.call-done = bf16[640,112]{1,0:T(8,128)(2,1)} async-done(((bf16[1280,112]{1,0:T(8,128)(2,1)}), bf16[640,112]{1,0:T(8,128)(2,1)}) %reduce-scatter.7.cloned.1.call-update) | async-done | bytes 143376
  305.1 1.1 copy.49
  306.2 2.0 all_gather.25
  308.2 56.6 %all-gather.15.cloned.1.call-done = bf16[1280,640]{1,0:T(8,128)(2,1)} async-done(((bf16[80,640]{1,0:T(8,128)(2,1)}), bf16[1280,640]{1,0:T(8,128)(2,1)}) %all-gather.15.cloned.1.call-update) | async-done | bytes 1638416 | tf_op jit(solution)/shard_map/all_gather | solution.py:89
  364.7 71.0 %all-gather.17.cloned.1.call-done = bf16[2,640,1280]{1,2,0:T(8,128)(2,1)} async-done(((bf16[2,640,80]{1,2,0:T(8,128)(2,1)}), bf16[2,640,1280]{1,2,0:T(8,128)(2,1)}) %all-gather.17.cloned.1.call-update) | async-done | bytes 3276816 | tf_op jit(solution)/shard_map/all_gather | solution.py:92
  435.8 2.9 fusion.1
  438.7 2.0 fusion
  440.7 0.9 copy.50
  441.6 8.2 %reduce-scatter.9.cloned.1.call-done = bf16[640,112]{1,0:T(8,128)(2,1)} async-done(((bf16[1280,112]{1,0:T(8,128)(2,1)}), bf16[640,112]{1,0:T(8,128)(2,1)}) %reduce-scatter.9.cloned.1.call-update) | async-done | bytes 143376
  449.8 1.1 copy.51
  450.9 0.7 convert_element_type.117
  (25 shorter events, 0.3 us)
Async XLA Ops:
  6.5 84.6 %all-gather.7.cloned.1.call-start = ((), (), s32[]{:S(2)}) async-start(), calls=%async_computation.2 | async-start | bytes 5222400 | tf_op jit(solution)/shard_map/all_gather | solution.py:40
  7.3 143.3 %all-gather.9.cloned.1.call-start = ((), (), s32[]{:S(2)}) async-start(), calls=%async_computation.3 | async-start | bytes 1740800 | tf_op jit(solution)/shard_map/all_gather | solution.py:72
  8.0 164.9 %all-reduce.2.cloned.1.call-start = ((), (), s32[]{:S(2)}) async-start(), calls=%async_computation.4 | async-start | bytes 573440 | tf_op jit(solution)/shard_map/psum | solution.py:74
  12.7 3.9 copy-start
  12.7 4.0 copy-start.5
  12.7 78.4 %copy-start.2 = (f32[1280]{0:T(1024)S(1)}, f32[1280]{0:T(1024)}, u32[]{:S(2)}) copy-start(f32[1280]{0:T(1024)} %param.17) | copy-start | bytes 15364
  95.4 2.8 copy-start.4
  99.3 3.5 copy-start.1
  150.6 141.5 %copy-start.3 = (f32[1280]{0:T(1024)S(1)}, f32[1280]{0:T(1024)}, u32[]{:S(2)}) copy-start(f32[1280]{0:T(1024)} %param.18) | copy-start | bytes 15364
  153.4 79.2 %all-gather.11.cloned.1.call-start = ((), (), s32[]{:S(2)}) async-start(), calls=%async_computation.5 | async-start | bytes 1740800 | tf_op jit(solution)/shard_map/all_gather | solution.py:76
  153.9 138.2 %all-gather.13.cloned.1.call-start = ((), (), s32[]{:S(2)}) async-start(), calls=%async_computation.6 | async-start | bytes 1740800 | tf_op jit(solution)/shard_map/all_gather | solution.py:80
  154.5 150.5 %reduce-scatter.7.cloned.1.call-start = ((), (), s32[]{:S(2)}) async-start(), calls=%async_computation.9 | async-start | bytes 491520
  296.0 68.7 %all-gather.15.cloned.1.call-start = ((), (), s32[]{:S(2)}) async-start(), calls=%async_computation.7 | async-start | bytes 1740800 | tf_op jit(solution)/shard_map/all_gather | solution.py:89
  296.8 139.0 %all-gather.17.cloned.1.call-start = ((), (), s32[]{:S(2)}) async-start(), calls=%async_computation.8 | async-start | bytes 3481600 | tf_op jit(solution)/shard_map/all_gather | solution.py:92
  297.5 152.3 %reduce-scatter.9.cloned.1.call-start = ((), (), s32[]{:S(2)}) async-start(), calls=%async_computation.10 | async-start | bytes 491520
Sparse Core Ops, SparseCore 0:
  10.0 81.0 all-gather.6
  93.8 56.7 all-gather.8
  153.5 19.3 all-reduce.1
  175.4 57.0 all-gather.10
  235.1 56.9 all-gather.12
  296.1 8.8 reduce-scatter.6
  307.7 56.9 all-gather.14
  367.5 68.2 all-gather.16
  441.7 8.0 reduce-scatter.8
where the time goes:
time: 460 us; the launch traced here: 458 us
  waiting for transfers between devices  404 us (88%)
  local copies, waits for them, and re-layouts  15.3 us (3%)
  matrix products  14.9 us (3%)
  between operations  13.4 us (3%)
  other arithmetic  8.44 us (2%)
    all_gather x1, waiting for transfers between devices, per_device(): combined_attend_triple = lax.all_gather(w_qkv, 'dp', axis=1, tiled=True)  74.4 us
    all_gather x1, waiting for transfers between devices, per_device(): shard_piece = lax.all_gather(final_layer_matrices, 'dp', axis=2, tiled=True)  71 us
    all_gather x1, waiting for transfers between devices, per_device(): lax.all_gather(w_down, 'dp', axis=1, tiled=True)  59.5 us
    all_gather x1, waiting for transfers between devices, per_device(): up_projection_full = lax.all_gather(w_up, 'dp', axis=0, tiled=True)  58.5 us
    all_gather x1, waiting for transfers between devices, per_device(): hidden_full = lax.all_gather(head_hidden, 'dp', axis=0, tiled=True)  56.6 us
    all_gather x1, waiting for transfers between devices, per_device(): lax.all_gather(w_out, 'dp', axis=1, tiled=True)  45.9 us
    unnamed x11, waiting for transfers between devices  19.6 us
    psum x1, waiting for transfers between devices, per_device(): lax.psum(attention.astype(jnp.bfloat16), 'mp').astype(jnp.float32)  18.3 us
  transfers between devices with their start and end apart: 9, of which 9 were waited for; matrix products, arithmetic and copies ran while one was open for 5% of the time, Pallas kernels for 0%

commit v1 on v0

v1 whole, which is shorter than its diff:
```python
import functools
import math

import jax
import jax.numpy as jnp
from jax import lax
from jax.experimental import pallas as pl
from jax.experimental.pallas import tpu as pltpu
from jax.sharding import PartitionSpec as P

MESH = pl.DeviceIdType.MESH


def grid_of(mesh):
    count = mesh.shape["dp"]
    try:
        coords = [tuple(d.coords) for d in mesh.devices[:, 0]]
        sizes = [len({c[k] for c in coords}) for k in (2, 1, 0)]
    except Exception:
        sizes = [count, 1, 1]
    if math.prod(sizes) != count:
        sizes = [count, 1, 1]
    return tuple(sizes)


def axis_orders(count):
    pattern = ((0, 1, 2), (0, 2, 1), (2, 1, 0), (0, 1, 2), (0, 2, 1), (0, 1, 2), (2, 1, 0), (0, 2, 1), (0, 1, 2))
    return [pattern[i % len(pattern)] for i in range(count)]


def gather_kernel(sizes, orders, own_ref, full_ref, local_sem, send_sem, recv_sem):
    me = lax.axis_index("dp")
    spans = (sizes[1] * sizes[2], sizes[2], 1)
    pos = tuple((me // spans[k]) % sizes[k] for k in range(3))

    def peer(axis, step):
        other = lax.rem(pos[axis] + step, sizes[axis])
        return me + (other - pos[axis]) * spans[axis]

    barrier = pltpu.get_barrier_semaphore()
    peers = [(axis, step) for axis in range(3) for step in range(1, sizes[axis])]
    for axis, step in peers:
        pl.semaphore_signal(barrier, inc=1, device_id={"dp": peer(axis, step)}, device_id_type=MESH)
    pl.semaphore_wait(barrier, len(peers))

    slot = {key: i for i, key in enumerate(peers)}

    def copies(m, phase):
        axis = orders[m][phase]
        done = orders[m][:phase]
        where = tuple(slice(None) if k in done else pos[k] for k in range(3))
        target = full_ref.at[(m,) + where]
        source = own_ref.at[m] if phase == 0 else target
        return [
            pltpu.make_async_remote_copy(
                src_ref=source,
                dst_ref=target,
                send_sem=send_sem.at[m, slot[axis, step]],
                recv_sem=recv_sem.at[m, slot[axis, step]],
                device_id={"dp": peer(axis, step)},
                device_id_type=MESH,
            )
            for step in range(1, sizes[axis])
        ]

    count = len(orders)
    flying = []
    local = []
    for m in range(count):
        flying.append(copies(m, 0))
        for copy in flying[m]:
            copy.start()
    for m in range(count):
        copy = pltpu.make_async_copy(own_ref.at[m], full_ref.at[(m,) + pos], local_sem.at[m])
        copy.start()
        local.append(copy)
    sent = []
    for phase in range(1, 3):
        for m in range(count):
            if phase == 1:
                local[m].wait()
            for copy in flying[m]:
                copy.wait_recv()
            sent += flying[m]
            flying[m] = copies(m, phase)
            for copy in flying[m]:
                copy.start()
    for m in range(count):
        for copy in flying[m]:
            copy.wait_recv()
        sent += flying[m]
    for copy in sent:
        copy.wait_send()


def gather_all(own, sizes):
    count, rows, columns = own.shape
    if rows % 16:
        return lax.all_gather(own, "dp", axis=1, tiled=True)
    slots = sum(size - 1 for size in sizes)
    full = pl.pallas_call(
        functools.partial(gather_kernel, sizes, axis_orders(count)),
        out_shape=jax.ShapeDtypeStruct((count,) + sizes + (rows, columns), own.dtype),
        in_specs=[pl.BlockSpec(memory_space=pltpu.VMEM)],
        out_specs=pl.BlockSpec(memory_space=pl.ANY),
        scratch_shapes=[
            pltpu.SemaphoreType.DMA((count,)),
            pltpu.SemaphoreType.DMA((count, slots)),
            pltpu.SemaphoreType.DMA((count, slots)),
        ],
        compiler_params=pltpu.CompilerParams(collective_id=0, has_side_effects=True),
        name="gather_weights",
    )(own)
    return full.reshape(count, math.prod(sizes) * rows, columns)


def swap(values):
    return lax.ppermute(values, "mp", [(0, 1), (1, 0)])


def rms_scale(values, gain):
    meansq = jnp.mean(values * values, axis=-1, keepdims=True)
    return values * lax.rsqrt(meansq + 1e-06) * gain


def dot_t(left, right):
    return lax.dot_general(
        left, right, (((1,), (1,)), ((), ())), preferred_element_type=jnp.float32
    )


def per_device(
    sizes,
    new_embed,
    context_key_cache,
    value_cache,
    valid,
    attn_gain,
    mlp_gain,
    query_scale,
    w_qkv,
    w_out,
    w_up,
    w_down,
    head_hidden,
    final_layer_matrices,
):
    row_count = new_embed.shape[0]
    context_len = context_key_cache.shape[1]
    local_width = context_key_cache.shape[2]
    head_size = query_scale.shape[0]
    local_heads = local_width // head_size
    mp_index = lax.axis_index("mp")
    own = jnp.concatenate(
        [
            w_qkv,
            w_out.T[None],
            w_up[None],
            w_down.T[None],
            head_hidden[None],
            jnp.swapaxes(final_layer_matrices, 1, 2),
        ],
        axis=0,
    )
    full = gather_all(own, sizes)
    stream = new_embed.astype(jnp.float32)
    normed = rms_scale(stream, attn_gain).astype(jnp.bfloat16)
    projected = [jnp.dot(normed, full[j], preferred_element_type=jnp.float32) for j in range(3)]
    query_all = projected[0].reshape(row_count, local_heads, head_size)
    query_all = (query_all * query_scale / math.sqrt(head_size)).astype(jnp.bfloat16)
    key_new = projected[1].astype(jnp.bfloat16).reshape(row_count, local_heads, head_size)
    value_new = projected[2].astype(jnp.bfloat16).reshape(row_count, local_heads, head_size)
    cache_keys = context_key_cache.reshape(row_count, context_len, local_heads, head_size)
    cache_vals = value_cache.reshape(row_count, context_len, local_heads, head_size)
    scores = jnp.einsum("bhe,bche->bhc", query_all, cache_keys, preferred_element_type=jnp.float32)
    own_score = jnp.sum(query_all.astype(jnp.float32) * key_new.astype(jnp.float32), axis=-1)
    in_use = jnp.arange(context_len, dtype=jnp.int32)[None, :] < valid[:, None]
    scores = jnp.where(in_use[:, None, :], scores, -jnp.inf)
    highest = jnp.maximum(jnp.max(scores, axis=-1), own_score)
    exp_cache = jnp.exp(scores - highest[..., None])
    exp_own = jnp.exp(own_score - highest)
    denominator = jnp.sum(exp_cache, axis=-1) + exp_own
    weight_cache = (exp_cache / denominator[..., None]).astype(jnp.bfloat16)
    weight_own = (exp_own / denominator).astype(jnp.bfloat16)
    context = jnp.einsum(
        "bhc,bche->bhe", weight_cache, cache_vals, preferred_element_type=jnp.float32
    )
    context = context + weight_own.astype(jnp.float32)[..., None] * value_new.astype(jnp.float32)
    context = context.astype(jnp.bfloat16).reshape(row_count, local_width)
    attention = dot_t(context, full[3]).astype(jnp.bfloat16)
    stream1 = stream + (attention.astype(jnp.float32) + swap(attention).astype(jnp.float32))
    normed2 = rms_scale(stream1, mlp_gain).astype(jnp.bfloat16)
    up_act = jnp.dot(normed2, full[4], preferred_element_type=jnp.float32)
    hidden = jax.nn.relu(up_act).astype(jnp.bfloat16)
    feed_out = dot_t(hidden, full[5]).astype(jnp.bfloat16)
    stream2 = stream1 + (feed_out.astype(jnp.float32) + swap(feed_out).astype(jnp.float32))
    stream2 = stream2.astype(jnp.bfloat16)
    half = final_layer_matrices.shape[1]
    stream_half = lax.dynamic_slice_in_dim(stream2, mp_index * half, half, 1)
    head_pre = jnp.dot(stream2, full[6], preferred_element_type=jnp.float32)
    head_act = jax.nn.silu(head_pre).astype(jnp.bfloat16)
    partial_out = dot_t(head_act, full[7]) + dot_t(stream_half, full[8])
    out_half = partial_out.shape[1] // 2
    mine = lax.dynamic_slice_in_dim(partial_out, mp_index * out_half, out_half, 1)
    theirs = lax.dynamic_slice_in_dim(partial_out, (1 - mp_index) * out_half, out_half, 1)
    return mine + swap(theirs.astype(jnp.bfloat16)).astype(jnp.float32)


def solution(mesh):
    in_specs = (
        P("dp", None),
        P("dp", None, "mp"),
        P("dp", None, "mp"),
        P("dp"),
        P(),
        P(),
        P(),
        P(None, "dp", "mp"),
        P("mp", "dp"),
        P("dp", "mp"),
        P("mp", "dp"),
        P("dp", "mp"),
        P(None, "mp", "dp"),
    )
    out_specs = P("dp", "mp")
    return jax.shard_map(
        functools.partial(per_device, grid_of(mesh)),
        mesh=mesh,
        in_specs=in_specs,
        out_specs=out_specs,
        check_vma=False,
    )
```

time: 460 us -> 193 us (0.42)
  waiting for transfers between devices: 404 us -> 3.4 us
  Pallas kernels: 0 us -> 144 us
  between operations: 13.4 us -> 0.27 us
  local copies, waits for them, and re-layouts: 15.3 us -> 27.4 us
    all_gather x6 -> x0, waiting for transfers between devices: 366 us -> none  [the longest x1 74.4 us: per_device(): combined_attend_triple = lax.all_gather(w_qkv, 'dp', axis=1, tiled=True)]
    pallas_call x0 -> x1, Pallas kernels: none -> 144 us  [gather_all(): pl.pallas_call(functools.partial(gather_kernel, sizes, axis_orders(count)...]
    unnamed x11 -> x0, waiting for transfers between devices: 19.6 us -> none
    psum x1 -> x0, waiting for transfers between devices: 18.3 us -> none  [per_device(): lax.psum(attention.astype(jnp.bfloat16), 'mp').astype(jnp.float32)]
    slice x2 -> x1, local copies, waits for them, and re-layouts: 1.88 us -> 9.94 us  [per_device(): partial_out = dot_t(head_act, full[7]) + dot_t(stream_half, full[8])]
    dot_general x5 -> x7, matrix products: 14.9 us -> 11.1 us  [the longest x4 6.6 us: dot_t(): lax.dot_general(left, right, (((1,), (1,)), ((), ())), preferred_element_...]
    unnamed x19 -> x26, local copies, waits for them, and re-layouts: 13.1 us -> 13.9 us
  transfers between devices with their start and end apart: 9 -> 3, of which waited for: 9 -> 3; matrix products, arithmetic and copies ran while one was open for 5% -> 0% of each run, Pallas kernels for 0% -> 0%
where the time goes in v1:
time: 193 us; the launch traced here: 192 us
  Pallas kernels  144 us (75%)
  local copies, waits for them, and re-layouts  27.4 us (14%)
  matrix products  11.1 us (6%)
  other arithmetic  4.21 us (2%)
  waiting for transfers between devices  3.4 us (2%)
  starting transfers between devices  2.1 us (1%)
    pallas_call x1, Pallas kernels, gather_all(): pl.pallas_call(functools.partial(gather_kernel, sizes, axis_orders(count)...  144 us
    unnamed x26, local copies, waits for them, and re-layouts  13.9 us
    slice x1, local copies, waits for them, and re-layouts, per_device(): partial_out = dot_t(head_act, full[7]) + dot_t(stream_half, full[8])  9.94 us
    dot_general x4, matrix products, dot_t(): lax.dot_general(left, right, (((1,), (1,)), ((), ())), preferred_element_...  6.6 us
    dot_general x3, matrix products, per_device(): jnp.dot(normed, full[j], preferred_element_type=jnp.float32)  4.46 us
  transfers between devices with their start and end apart: 3, of which 3 were waited for; matrix products, arithmetic and copies ran while one was open for 0% of the time, Pallas kernels for 0%

profile of v1, /device:TPU:13, one launch (start us, length us, event | category | flops | bytes accessed | tf_op | source)
XLA Modules:
  0.0 192.4 jit_solution(15513270022722503910)
XLA Ops:
  0.0 1.0 constant_dynamic-update-slice_fusion
  1.0 0.9 bitcast_dynamic-update-slice_fusion.2
  1.9 0.9 bitcast_dynamic-update-slice_fusion.4
  2.8 0.9 bitcast_dynamic-update-slice_fusion.1
  3.7 0.9 bitcast_dynamic-update-slice_fusion.3
  4.7 1.0 bitcast_dynamic-update-slice_fusion.own_ref
  5.6 0.0 copy-start.4
  5.6 0.9 copy-done.4
  6.5 144.0 %gather_weights.1 = bf16[9,4,2,2,80,640]{5,4,3,2,1,0:T(8,128)(2,1)} custom-call(bf16[9,80,640]{2,1,0:T(8,128)(2,1)} %copy-done.4), custom_call_target="tpu_custom_call" | custom-call | tf_op jit(solution)/shard_map/gather_weights/pallas_call | solution.py:101
  150.5 0.0 copy-start
  150.6 0.0 copy-start.5
  150.6 9.9 %fusion.29 = (bf16[1,4,2,2,80,640]{5,4,3,2,1,0:T(8,128)(2,1)}, bf16[1,4,2,2,80,640]{5,4,3,2,1,0:T(8,128)(2,1)}, bf16[1,4,2,2,80,640]{5,4,3,2,1,0:T(8,128)(2,1)},...) fusion(bf16[9,4,2,2,80,640]{5,4,3,2,1,0:T(8,128)(2,1)} %gather_, ...), kind=kLoop, calls=%fused_computation.58 | loop fusion | bytes 29491200 | tf_op jit(solution)/shard_map/slice | solution.py:202
  160.5 0.0 copy-done
  160.5 0.1 fusion.6
  160.7 0.0 copy-done.5
  160.7 0.5 fusion.5
  161.2 0.2 copy.25
  161.3 2.2 %copy.23 = bf16[640,1280]{1,0:T(8,128)(2,1)} copy(bf16[640,1280]{0,1:T(8,128)(2,1)S(1)} %bitcast.60) | data formatting | bytes 3276800 | tf_op jit(solution)/shard_map/dot_general | solution.py:168
  163.5 3.8 %copy.41 = bf16[112,16,640]{0,2,1:T(8,128)(2,1)S(1)} copy(bf16[112,16,640]{2,1,0:T(8,128)(2,1)} %param.14) | data formatting | bytes 4587520
  167.4 0.0 copy-done.8
  167.4 0.0 copy-done.7
  167.4 2.1 %multiply_reduce_fusion.3 = (f32[112,8]{0,1:T(8,128)S(1)}, f32[112,8,80]{0,2,1:T(8,128)S(1)}) fusion(f32[112,8,80]{0,2,1:T(8,128)S(1)} %bitcast.65, f32[80]{0:T(128)S(1)} %copy-done.7, bf16[8,80,1280]{2,1,0:T(8,128)(2,1)} %bitcast.62, f32[1280]{0:T(1024)S(1)} %copy-done.5, f32[112]{0:T(128)S(1)} %add_rsqrt_fusion.1, bf16[112,1280]{1,0:T(8,128)(2,1)S(1)} %copy-done), kind=kOutput, calls=%fused_computation.25 | convolution fusion | flops 184503424 | bytes 2508032 | tf_op jit(solution)/shard_map/dot_general | solution.py:168
  169.5 0.9 multiply_reduce_fusion.1
  170.6 0.7 copy.44
  171.3 3.8 %copy.42 = bf16[112,16,640]{0,2,1:T(8,128)(2,1)S(1)} copy(bf16[112,16,640]{2,1,0:T(8,128)(2,1)} %param.15) | data formatting | bytes 4587520
  175.1 1.9 fusion.4
  177.0 0.2 copy.27
  177.2 0.0 copy-start.3
  177.2 1.8 multiply_reduce_fusion
  179.0 0.1 add_convert_fusion.1
  179.0 0.0 copy-start.2
  179.0 0.0 copy-start.6
  179.0 0.0 copy-done.3
  179.1 0.6 convolution_convert_fusion.1
  179.7 1.2 collective-permute-start
  180.9 1.2 collective-permute-done
  182.1 0.2 multiply_reduce_fusion.2
  182.3 0.0 copy-done.2
  182.3 0.0 copy-done.6
  182.3 2.4 %convolution_convert_fusion = bf16[112,1280]{1,0:T(8,128)(2,1)S(1)} fusion(bf16[1280,640]{1,0:T(8,128)(2,1)S(1)} %bitcast.56, bf16[1280,640]{1,0:T(8,128)(2,1)} %bitcast.57, f32[1280]{0:T(1024)S(1)} %copy-done.6, f32[112]{0:T(128)S(1)} %add_rsqrt_fusion, bf16[112,1280]{1,0:T(8,128)(2,1)S(1)} %copy-done, bf16[112,1280]{1,0:T(8,128)(2,1)S(1)} %collective-permute-done, ...), kind=kOutput, calls=%fused_computation.3 | convolution fusion | flops 368435200 | bytes 4429248 | tf_op jit(solution)/shard_map/dot_general | solution.py:127
  184.8 0.4 collective-permute-start.1
  185.2 1.2 collective-permute-done.1
  186.4 0.2 add_convert_fusion
  186.6 3.0 %fusion.14 = f32[112,1280]{1,0:T(8,128)S(1)} fusion(bf16[1280,640]{1,0:T(8,128)(2,1)} %bitcast.63, bf16[112,1280]{1,0:T(8,128)(2,1)S(1)} %add_convert_fusion, bf16[1280,640]{1,0:T(8,128)(2,1)} %bitcast.64), kind=kOutput, calls=%fused_computation.33 | convolution fusion | flops 367360000 | bytes 4136960 | tf_op jit(solution)/shard_map/dot_general | solution.py:127
  189.6 0.6 convolution_add_fusion
  190.2 0.4 collective-permute-start.2
  190.7 1.0 collective-permute-done.2
  191.7 0.7 convert_add_fusion.1
  (13 shorter events, 0.2 us)
Async XLA Ops:
  5.6 0.9 copy-start.4
  150.5 10.0 %copy-start = (bf16[112,1280]{1,0:T(8,128)(2,1)S(1)}, bf16[112,1280]{1,0:T(8,128)(2,1)}, u32[]{:S(2)}) copy-start(bf16[112,1280]{1,0:T(8,128)(2,1)} %param.13) | copy-start | bytes 860164
  150.6 10.1 %copy-start.5 = (f32[1280]{0:T(1024)S(1)}, f32[1280]{0:T(1024)}, u32[]{:S(2)}) copy-start(f32[1280]{0:T(1024)} %param.17) | copy-start | bytes 15364
  163.5 3.9 %copy-start.8 = (s32[112]{0:T(128)S(1)}, s32[112]{0:T(128)}, u32[]{:S(2)}) copy-start(s32[112]{0:T(128)} %param.16) | copy-start | bytes 1348
  163.5 3.9 %copy-start.7 = (f32[80]{0:T(128)S(1)}, f32[80]{0:T(128)}, u32[]{:S(2)}) copy-start(f32[80]{0:T(128)} %param.19) | copy-start | bytes 964
  177.2 1.9 copy-start.3
  179.0 3.3 %copy-start.2 = (bf16[1,4,2,2,80,640]{5,4,3,2,1,0:T(8,128)(2,1)S(1)}, bf16[1,4,2,2,80,640]{5,4,3,2,1,0:T(8,128)(2,1)}, u32[]{:S(2)}) copy-start(bf16[1,4,2,2,80,640]{5,4,3,2,1,0:T(8,128)(2,1)} %get-tuple-element.8) | copy-start | bytes 4915204
  179.0 3.3 %copy-start.6 = (f32[1280]{0:T(1024)S(1)}, f32[1280]{0:T(1024)}, u32[]{:S(2)}) copy-start(f32[1280]{0:T(1024)} %param.18) | copy-start | bytes 15364
  179.7 2.4 %collective-permute-start = (bf16[112,1280]{1,0:T(8,128)(2,1)S(1)}, bf16[112,1280]{1,0:T(8,128)(2,1)S(1)}, u32[]{:S(2)}, u32[]{:S(2)}) collective-permute-start(bf16[112,1280]{1,0:T(8,128)(2,1)S(1)} %convolution_convert_fusion.1), channel_id=1, source_target_pairs={{0,1},{1,0},{2,3},{3,2},{4,5},{5,4},{6,7},{7,6},{8,9},{9,8},{10,11... | collective-permute-start | bytes 860168 | tf_op jit(solution)/shard_map/ppermute | solution.py:118
  184.8 1.6 collective-permute-start.1
  186.6 3.0 %copy-start.1 = (bf16[1,4,2,2,80,640]{5,4,3,2,1,0:T(8,128)(2,1)S(1)}, bf16[1,4,2,2,80,640]{5,4,3,2,1,0:T(8,128)(2,1)}, u32[]{:S(2)}) copy-start(bf16[1,4,2,2,80,640]{5,4,3,2,1,0:T(8,128)(2,1)} %get-tuple-element.5) | copy-start | bytes 4915204
  190.2 1.4 collective-permute-start.2

commit v2 on v1

--- a/solution.py
+++ b/solution.py
@@ -24,11 +24,14 @@
 
 
 def axis_orders(count):
-    pattern = ((0, 1, 2), (0, 2, 1), (2, 1, 0), (0, 1, 2), (0, 2, 1), (0, 1, 2), (2, 1, 0), (0, 2, 1), (0, 1, 2))
-    return [pattern[i % len(pattern)] for i in range(count)]
-
-
-def gather_kernel(sizes, orders, own_ref, full_ref, local_sem, send_sem, recv_sem):
+    pair = ((0, 1, 2), (0, 2, 1))
+    return [pair[m % 2] for m in range(count - 1)] + [(2, 1, 0)]
+
+
+def gather_kernel(sizes, orders, own_counts, *refs):
+    own_refs = refs[: len(own_counts)]
+    full_ref, local_sem, send_sem, recv_sem = refs[len(own_counts) :]
+    blocks = [ref.at[i] for ref, n in zip(own_refs, own_counts) for i in range(n)]
     me = lax.axis_index("dp")
     spans = (sizes[1] * sizes[2], sizes[2], 1)
     pos = tuple((me // spans[k]) % sizes[k] for k in range(3))
@@ -50,7 +53,7 @@
         done = orders[m][:phase]
         where = tuple(slice(None) if k in done else pos[k] for k in range(3))
         target = full_ref.at[(m,) + where]
-        source = own_ref.at[m] if phase == 0 else target
+        source = blocks[m] if phase == 0 else target
         return [
             pltpu.make_async_remote_copy(
                 src_ref=source,
@@ -64,44 +67,53 @@
         ]
 
     count = len(orders)
-    flying = []
+    flying = [None] * count
+    sent = []
+
+    def begin(m, phase):
+        if phase:
+            for copy in flying[m]:
+                copy.wait_recv()
+            sent.extend(flying[m])
+        flying[m] = copies(m, phase)
+        for copy in flying[m]:
+            copy.start()
+
+    for m in [0, count - 1] + list(range(1, count - 1)):
+        begin(m, 0)
     local = []
     for m in range(count):
-        flying.append(copies(m, 0))
-        for copy in flying[m]:
-            copy.start()
-    for m in range(count):
-        copy = pltpu.make_async_copy(own_ref.at[m], full_ref.at[(m,) + pos], local_sem.at[m])
+        copy = pltpu.make_async_copy(blocks[m], full_ref.at[(m,) + pos], local_sem.at[m])
         copy.start()
         local.append(copy)
-    sent = []
-    for phase in range(1, 3):
-        for m in range(count):
-            if phase == 1:
-                local[m].wait()
-            for copy in flying[m]:
-                copy.wait_recv()
-            sent += flying[m]
-            flying[m] = copies(m, phase)
-            for copy in flying[m]:
-                copy.start()
+    for copy in local:
+        copy.wait()
+    begin(count - 1, 1)
+    begin(count - 1, 2)
+    for m in range(count):
+        if m < count - 1:
+            begin(m, 1)
+        if m >= 1:
+            begin(m - 1, 2)
     for m in range(count):
         for copy in flying[m]:
             copy.wait_recv()
-        sent += flying[m]
+        sent.extend(flying[m])
     for copy in sent:
         copy.wait_send()
 
 
-def gather_all(own, sizes):
-    count, rows, columns = own.shape
+def gather_all(owns, sizes):
+    rows, columns = owns[0].shape[1:]
+    counts = [own.shape[0] for own in owns]
+    count = sum(counts)
     if rows % 16:
-        return lax.all_gather(own, "dp", axis=1, tiled=True)
+        return lax.all_gather(jnp.concatenate(owns, axis=0), "dp", axis=1, tiled=True)
     slots = sum(size - 1 for size in sizes)
     full = pl.pallas_call(
-        functools.partial(gather_kernel, sizes, axis_orders(count)),
-        out_shape=jax.ShapeDtypeStruct((count,) + sizes + (rows, columns), own.dtype),
-        in_specs=[pl.BlockSpec(memory_space=pltpu.VMEM)],
+        functools.partial(gather_kernel, sizes, axis_orders(count), counts),
+        out_shape=jax.ShapeDtypeStruct((count,) + sizes + (rows, columns), owns[0].dtype),
+        in_specs=[pl.BlockSpec(memory_space=pltpu.VMEM)] * len(owns),
         out_specs=pl.BlockSpec(memory_space=pl.ANY),
         scratch_shapes=[
             pltpu.SemaphoreType.DMA((count,)),
@@ -110,7 +122,7 @@
         ],
         compiler_params=pltpu.CompilerParams(collective_id=0, has_side_effects=True),
         name="gather_weights",
-    )(own)
+    )(*owns)
     return full.reshape(count, math.prod(sizes) * rows, columns)
 
 
@@ -151,18 +163,15 @@
     head_size = query_scale.shape[0]
     local_heads = local_width // head_size
     mp_index = lax.axis_index("mp")
-    own = jnp.concatenate(
-        [
-            w_qkv,
-            w_out.T[None],
-            w_up[None],
-            w_down.T[None],
-            head_hidden[None],
-            jnp.swapaxes(final_layer_matrices, 1, 2),
-        ],
-        axis=0,
-    )
-    full = gather_all(own, sizes)
+    owns = [
+        w_qkv,
+        w_out.T[None],
+        w_up[None],
+        w_down.T[None],
+        head_hidden[None],
+        jnp.swapaxes(final_layer_matrices, 1, 2),
+    ]
+    full = gather_all(owns, sizes)
     stream = new_embed.astype(jnp.float32)
     normed = rms_scale(stream, attn_gain).astype(jnp.bfloat16)
     projected = [jnp.dot(normed, full[j], preferred_element_type=jnp.float32) for j in range(3)]

time: 193 us -> 195 us (1.010)
  local copies, waits for them, and re-layouts: 27.4 us -> 20.9 us
  Pallas kernels: 144 us -> 149 us
    unnamed x26 -> x19, local copies, waits for them, and re-layouts: 13.9 us -> 8.35 us
    pallas_call x1, Pallas kernels: 144 us -> 149 us  [gather_all(): pl.pallas_call(functools.partial(gather_kernel, sizes, axis_orders(count)...]
where the time goes in v2:
time: 195 us; the launch traced here: 193 us
  Pallas kernels  149 us (76%)
  local copies, waits for them, and re-layouts  20.9 us (11%)
  matrix products  11.1 us (6%)
  other arithmetic  4.21 us (2%)
  starting transfers between devices  4.02 us (2%)
  waiting for transfers between devices  3.4 us (2%)
    pallas_call x1, Pallas kernels, gather_all(): pl.pallas_call(functools.partial(gather_kernel, sizes, axis_orders(count)...  149 us
    slice x1, local copies, waits for them, and re-layouts, per_device(): partial_out = dot_t(head_act, full[7]) + dot_t(stream_half, full[8])  9.94 us
    unnamed x19, local copies, waits for them, and re-layouts  8.35 us
    dot_general x4, matrix products, dot_t(): lax.dot_general(left, right, (((1,), (1,)), ((), ())), preferred_element_...  6.6 us
    dot_general x3, matrix products, per_device(): jnp.dot(normed, full[j], preferred_element_type=jnp.float32)  4.46 us
    ppermute x3, starting transfers between devices, swap(): return lax.ppermute(values, 'mp', [(0, 1), (1, 0)])  4.02 us
  transfers between devices with their start and end apart: 3, of which 3 were waited for; matrix products, arithmetic and copies ran while one was open for 0% of the time, Pallas kernels for 0%

profile of v2, /device:TPU:13, one launch (start us, length us, event | category | flops | bytes accessed | tf_op | source)
XLA Modules:
  0.0 192.8 jit_solution(11303523751890157220)
XLA Ops:
  0.0 149.0 %gather_weights.1 = bf16[9,4,2,2,80,640]{5,4,3,2,1,0:T(8,128)(2,1)} custom-call(bf16[3,80,640]{2,1,0:T(8,128)(2,1)} %refs_0_.1, bf16[1,80,640]{2,1,0:T(8,128)(2,1)} %bitcast.64, bf16[1,80,640]{2,1,0:T(8,128)(2,1)} %bitcast.65, bf16[1,80,640]{2,1,0:T(8,128)(2,1)} %bitcast.66, bf16[1,80,640]{2,1,0:T(8,128)(2,1)} %bitcast.67, bf16[2,80,640]{2,1,0:T(8,128)(2,1)} %bitcast.63), custom_call_target="tpu_custom_call" | custom-call | tf_op jit(solution)/shard_map/gather_weights/pallas_call | solution.py:113
  149.0 0.0 copy-start
  149.0 0.0 copy-start.4
  149.1 9.9 %fusion.29 = (bf16[1,4,2,2,80,640]{5,4,3,2,1,0:T(8,128)(2,1)}, bf16[1,4,2,2,80,640]{5,4,3,2,1,0:T(8,128)(2,1)}, bf16[1,4,2,2,80,640]{5,4,3,2,1,0:T(8,128)(2,1)},...) fusion(bf16[9,4,2,2,80,640]{5,4,3,2,1,0:T(8,128)(2,1)} %gather_, ...), kind=kLoop, calls=%fused_computation.52 | loop fusion | bytes 29491200 | tf_op jit(solution)/shard_map/slice | solution.py:211
  159.0 0.0 copy-done
  159.0 0.1 fusion.6
  159.2 0.0 copy-done.4
  159.2 0.5 fusion.5
  159.6 0.2 copy.25
  159.8 2.2 %copy.23 = bf16[640,1280]{1,0:T(8,128)(2,1)} copy(bf16[640,1280]{0,1:T(8,128)(2,1)S(1)} %bitcast.55) | data formatting | bytes 3276800 | tf_op jit(solution)/shard_map/dot_general | solution.py:177
  162.0 0.0 copy-start.7
  162.0 0.0 copy-start.6
  162.0 3.8 %copy.41 = bf16[112,16,640]{0,2,1:T(8,128)(2,1)S(1)} copy(bf16[112,16,640]{2,1,0:T(8,128)(2,1)} %param.14) | data formatting | bytes 4587520
  165.9 0.0 copy-done.7
  165.9 0.0 copy-done.6
  165.9 2.1 %multiply_reduce_fusion.3 = (f32[112,8]{0,1:T(8,128)S(1)}, f32[112,8,80]{0,2,1:T(8,128)S(1)}) fusion(f32[112,8,80]{0,2,1:T(8,128)S(1)} %bitcast.60, f32[80]{0:T(128)S(1)} %copy-done.6, bf16[8,80,1280]{2,1,0:T(8,128)(2,1)} %bitcast.57, f32[1280]{0:T(1024)S(1)} %copy-done.4, f32[112]{0:T(128)S(1)} %add_rsqrt_fusion.1, bf16[112,1280]{1,0:T(8,128)(2,1)S(1)} %copy-done), kind=kOutput, calls=%fused_computation.25 | convolution fusion | flops 184503424 | bytes 2508032 | tf_op jit(solution)/shard_map/dot_general | solution.py:177
  168.0 0.9 multiply_reduce_fusion.1
  169.1 0.7 copy.44
  169.8 3.8 %copy.42 = bf16[112,16,640]{0,2,1:T(8,128)(2,1)S(1)} copy(bf16[112,16,640]{2,1,0:T(8,128)(2,1)} %param.15) | data formatting | bytes 4587520
  173.6 1.9 fusion.4
  175.5 0.2 copy.27
  175.7 0.0 copy-start.3
  175.7 1.8 multiply_reduce_fusion
  177.5 0.1 add_convert_fusion.1
  177.5 0.0 copy-start.2
  177.5 0.0 copy-start.5
  177.5 0.0 copy-done.3
  177.5 0.6 convolution_convert_fusion.1
  178.1 3.1 %collective-permute-start = (bf16[112,1280]{1,0:T(8,128)(2,1)S(1)}, bf16[112,1280]{1,0:T(8,128)(2,1)S(1)}, u32[]{:S(2)}, u32[]{:S(2)}) collective-permute-start(bf16[112,1280]{1,0:T(8,128)(2,1)S(1)} %convolution_convert_fusion.1), channel_id=1, source_target_pairs={{0,1},{1,0},{2,3},{3,2},{4,5},{5,4},{6,7},{7,6},{8,9},{9,8},{10,11... | collective-permute-start | bytes 860168 | tf_op jit(solution)/shard_map/ppermute | solution.py:130
  181.3 1.2 collective-permute-done
  182.5 0.2 multiply_reduce_fusion.2
  182.7 0.0 copy-done.2
  182.7 0.0 copy-done.5
  182.7 2.4 %convolution_convert_fusion = bf16[112,1280]{1,0:T(8,128)(2,1)S(1)} fusion(bf16[1280,640]{1,0:T(8,128)(2,1)S(1)} %bitcast.51, bf16[1280,640]{1,0:T(8,128)(2,1)} %bitcast.52, f32[1280]{0:T(1024)S(1)} %copy-done.5, f32[112]{0:T(128)S(1)} %add_rsqrt_fusion, bf16[112,1280]{1,0:T(8,128)(2,1)S(1)} %copy-done, bf16[112,1280]{1,0:T(8,128)(2,1)S(1)} %collective-permute-done, ...), kind=kOutput, calls=%fused_computation.3 | convolution fusion | flops 368435200 | bytes 4429248 | tf_op jit(solution)/shard_map/dot_general | solution.py:139
  185.2 0.4 collective-permute-start.1
  185.6 1.2 collective-permute-done.1
  186.8 0.2 add_convert_fusion
  187.0 0.0 copy-start.1
  187.0 3.0 %fusion.14 = f32[112,1280]{1,0:T(8,128)S(1)} fusion(bf16[1280,640]{1,0:T(8,128)(2,1)} %bitcast.58, bf16[112,1280]{1,0:T(8,128)(2,1)S(1)} %add_convert_fusion, bf16[1280,640]{1,0:T(8,128)(2,1)} %bitcast.59), kind=kOutput, calls=%fused_computation.32 | convolution fusion | flops 367360000 | bytes 4136960 | tf_op jit(solution)/shard_map/dot_general | solution.py:139
  190.0 0.0 copy-done.1
  190.0 0.6 convolution_add_fusion
  190.6 0.4 collective-permute-start.2
  191.1 1.0 collective-permute-done.2
  192.1 0.7 convert_add_fusion.1
  (9 shorter events, 0.2 us)
Async XLA Ops:
  149.0 10.0 %copy-start = (bf16[112,1280]{1,0:T(8,128)(2,1)S(1)}, bf16[112,1280]{1,0:T(8,128)(2,1)}, u32[]{:S(2)}) copy-start(bf16[112,1280]{1,0:T(8,128)(2,1)} %param.13) | copy-start | bytes 860164
  149.0 10.1 %copy-start.4 = (f32[1280]{0:T(1024)S(1)}, f32[1280]{0:T(1024)}, u32[]{:S(2)}) copy-start(f32[1280]{0:T(1024)} %param.17) | copy-start | bytes 15364
  162.0 3.9 %copy-start.7 = (s32[112]{0:T(128)S(1)}, s32[112]{0:T(128)}, u32[]{:S(2)}) copy-start(s32[112]{0:T(128)} %param.16) | copy-start | bytes 1348
  162.0 3.9 %copy-start.6 = (f32[80]{0:T(128)S(1)}, f32[80]{0:T(128)}, u32[]{:S(2)}) copy-start(f32[80]{0:T(128)} %param.19) | copy-start | bytes 964
  175.7 1.9 copy-start.3
  177.5 5.2 %copy-start.2 = (bf16[1,4,2,2,80,640]{5,4,3,2,1,0:T(8,128)(2,1)S(1)}, bf16[1,4,2,2,80,640]{5,4,3,2,1,0:T(8,128)(2,1)}, u32[]{:S(2)}) copy-start(bf16[1,4,2,2,80,640]{5,4,3,2,1,0:T(8,128)(2,1)} %get-tuple-element.8) | copy-start | bytes 4915204
  177.5 5.2 %copy-start.5 = (f32[1280]{0:T(1024)S(1)}, f32[1280]{0:T(1024)}, u32[]{:S(2)}) copy-start(f32[1280]{0:T(1024)} %param.18) | copy-start | bytes 15364
  178.1 4.3 %collective-permute-start = (bf16[112,1280]{1,0:T(8,128)(2,1)S(1)}, bf16[112,1280]{1,0:T(8,128)(2,1)S(1)}, u32[]{:S(2)}, u32[]{:S(2)}) collective-permute-start(bf16[112,1280]{1,0:T(8,128)(2,1)S(1)} %convolution_convert_fusion.1), channel_id=1, source_target_pairs={{0,1},{1,0},{2,3},{3,2},{4,5},{5,4},{6,7},{7,6},{8,9},{9,8},{10,11... | collective-permute-start | bytes 860168 | tf_op jit(solution)/shard_map/ppermute | solution.py:130
  185.2 1.6 collective-permute-start.1
  187.0 3.0 %copy-start.1 = (bf16[1,4,2,2,80,640]{5,4,3,2,1,0:T(8,128)(2,1)S(1)}, bf16[1,4,2,2,80,640]{5,4,3,2,1,0:T(8,128)(2,1)}, u32[]{:S(2)}) copy-start(bf16[1,4,2,2,80,640]{5,4,3,2,1,0:T(8,128)(2,1)} %get-tuple-element.5) | copy-start | bytes 4915204
  190.6 1.4 collective-permute-start.2

commit v3 on v2

--- a/solution.py
+++ b/solution.py
@@ -28,11 +28,50 @@
     return [pair[m % 2] for m in range(count - 1)] + [(2, 1, 0)]
 
 
-def gather_kernel(sizes, orders, own_counts, *refs):
-    own_refs = refs[: len(own_counts)]
-    full_ref, local_sem, send_sem, recv_sem = refs[len(own_counts) :]
-    blocks = [ref.at[i] for ref, n in zip(own_refs, own_counts) for i in range(n)]
+def block_kernel(
+    sizes,
+    head_size,
+    x_ref,
+    key_ref,
+    value_ref,
+    valid_ref,
+    attn_gain_ref,
+    mlp_gain_ref,
+    scale_ref,
+    spread_ref,
+    heads_ref,
+    w_qkv_ref,
+    w_out_ref,
+    w_up_ref,
+    w_down_ref,
+    head_ref,
+    final_ref,
+    out_ref,
+    full_ref,
+    key_buf,
+    value_buf,
+    query_buf,
+    fresh_buf,
+    context_buf,
+    swap_out,
+    swap_in,
+    half_bf,
+    half_f32,
+    part_bf,
+    part_in,
+    cache_sem,
+    local_sem,
+    send_sem,
+    recv_sem,
+    swap_send,
+    swap_recv,
+):
+    own = [w_qkv_ref.at[j] for j in range(3)]
+    own += [w_out_ref, w_up_ref, w_down_ref, head_ref, final_ref.at[0], final_ref.at[1]]
+    count = len(own)
+    orders = axis_orders(count)
     me = lax.axis_index("dp")
+    mp = lax.axis_index("mp")
     spans = (sizes[1] * sizes[2], sizes[2], 1)
     pos = tuple((me // spans[k]) % sizes[k] for k in range(3))
 
@@ -40,23 +79,25 @@
         other = lax.rem(pos[axis] + step, sizes[axis])
         return me + (other - pos[axis]) * spans[axis]
 
+    cache_copies = [
+        pltpu.make_async_copy(key_ref, key_buf, cache_sem.at[0]),
+        pltpu.make_async_copy(value_ref, value_buf, cache_sem.at[1]),
+    ]
     barrier = pltpu.get_barrier_semaphore()
     peers = [(axis, step) for axis in range(3) for step in range(1, sizes[axis])]
     for axis, step in peers:
         pl.semaphore_signal(barrier, inc=1, device_id={"dp": peer(axis, step)}, device_id_type=MESH)
-    pl.semaphore_wait(barrier, len(peers))
-
+    pl.semaphore_signal(barrier, inc=1, device_id={"mp": 1 - mp}, device_id_type=MESH)
+    pl.semaphore_wait(barrier, len(peers) + 1)
     slot = {key: i for i, key in enumerate(peers)}
 
     def copies(m, phase):
         axis = orders[m][phase]
         done = orders[m][:phase]
-        where = tuple(slice(None) if k in done else pos[k] for k in range(3))
-        target = full_ref.at[(m,) + where]
-        source = blocks[m] if phase == 0 else target
+        target = full_ref.at[(m,) + tuple(slice(None) if k in done else pos[k] for k in range(3))]
         return [
             pltpu.make_async_remote_copy(
-                src_ref=source,
+                src_ref=target if phase else own[m],
                 dst_ref=target,
                 send_sem=send_sem.at[m, slot[axis, step]],
                 recv_sem=recv_sem.at[m, slot[axis, step]],
@@ -66,64 +107,229 @@
             for step in range(1, sizes[axis])
         ]
 
-    count = len(orders)
     flying = [None] * count
     sent = []
 
+    def arrive(m):
+        for copy in flying[m]:
+            copy.wait_recv()
+        sent.extend(flying[m])
+
     def begin(m, phase):
         if phase:
-            for copy in flying[m]:
-                copy.wait_recv()
-            sent.extend(flying[m])
+            arrive(m)
         flying[m] = copies(m, phase)
         for copy in flying[m]:
             copy.start()
 
-    for m in [0, count - 1] + list(range(1, count - 1)):
+    ahead = 3
+    for m in [0, count - 1] + list(range(1, ahead)):
         begin(m, 0)
     local = []
     for m in range(count):
-        copy = pltpu.make_async_copy(blocks[m], full_ref.at[(m,) + pos], local_sem.at[m])
+        copy = pltpu.make_async_copy(own[m], full_ref.at[(m,) + pos], local_sem.at[m])
         copy.start()
         local.append(copy)
+    for copy in cache_copies:
+        copy.start()
     for copy in local:
         copy.wait()
     begin(count - 1, 1)
-    begin(count - 1, 2)
-    for m in range(count):
-        if m < count - 1:
-            begin(m, 1)
+
+    def weight(m):
+        held = full_ref[m]
+        return held.reshape(math.prod(held.shape[:-1]), held.shape[-1])
+
+    def straight(left, m):
+        return jnp.dot(left, weight(m), preferred_element_type=jnp.float32)
+
+    def exchange(index, values):
+        swap_out[index] = values
+        copy = pltpu.make_async_remote_copy(
+            src_ref=swap_out.at[index],
+            dst_ref=swap_in.at[index],
+            send_sem=swap_send.at[index],
+            recv_sem=swap_recv.at[index],
+            device_id={"mp": 1 - mp},
+            device_id_type=MESH,
+        )
+        copy.start()
+        copy.wait()
+        return values.astype(jnp.float32) + swap_in[index].astype(jnp.float32)
+
+    def attend():
+        normed = rms_scale(x_ref[...].astype(jnp.float32), attn_gain_ref[...])
+        normed = normed.astype(jnp.bfloat16)
+        query = straight(normed, 0) * scale_ref[...] / math.sqrt(head_size)
+        query_buf[...] = query.astype(jnp.bfloat16)
+        fresh_buf[0] = straight(normed, 1).astype(jnp.bfloat16)
+        fresh_buf[1] = straight(normed, 2).astype(jnp.bfloat16)
+        for copy in cache_copies:
+            copy.wait()
+        rows = spread_ref.shape[1]
+        slots = spread_ref.shape[0]
+        context_len = slots // rows
+
+        def to_heads(product):
+            high = product.astype(jnp.bfloat16)
+            low = (product - high.astype(jnp.float32)).astype(jnp.bfloat16)
+            return dot_t(high, heads_ref[...]) + dot_t(low, heads_ref[...])
+
+        def from_heads(weights):
+            return jnp.dot(weights, heads_ref[...], preferred_element_type=jnp.float32)
+
+        def chunk(i, carry):
+            at = pl.ds(pl.multiple_of(i * rows, rows), rows)
+            wide = pl.ds(pl.multiple_of(i * slots, slots), slots)
+            query = query_buf[at, :]
+            spread = spread_ref[...]
+            query_rep = jnp.dot(spread, query, preferred_element_type=jnp.float32)
+            scores = to_heads(query_rep * key_buf[wide, :].astype(jnp.float32))
+            own_score = to_heads(
+                query.astype(jnp.float32) * fresh_buf[0, at, :].astype(jnp.float32)
+            )
+            limit = jnp.dot(spread, valid_ref[at, :], preferred_element_type=jnp.float32)
+            lanes = scores.shape[1]
+            scores = scores.reshape(rows, context_len, lanes)
+            place = lax.broadcasted_iota(jnp.int32, scores.shape, 1).astype(jnp.float32)
+            scores = jnp.where(place < limit.reshape(scores.shape), scores, -jnp.inf)
+            highest = jnp.maximum(jnp.max(scores, axis=1), own_score)
+            exp_cache = jnp.exp(scores - highest[:, None, :])
+            exp_own = jnp.exp(own_score - highest)
+            total = jnp.sum(exp_cache, axis=1) + exp_own
+            weight_cache = (exp_cache / total[:, None, :]).astype(jnp.bfloat16)
+            weight_own = (exp_own / total).astype(jnp.bfloat16)
+            mixed = from_heads(weight_cache.reshape(slots, lanes))
+            mixed = mixed * value_buf[wide, :].astype(jnp.float32)
+            mixed = jnp.sum(mixed.reshape(rows, context_len, mixed.shape[1]), axis=1)
+            mixed = mixed + from_heads(weight_own) * fresh_buf[1, at, :].astype(jnp.float32)
+            context_buf[at, :] = mixed.astype(jnp.bfloat16)
+            return carry
+
+        lax.fori_loop(0, query_buf.shape[0] // rows, chunk, 0)
+
+    for m in range(count - 1):
+        begin(m, 1)
+        if m + ahead < count - 1:
+            begin(m + ahead, 0)
         if m >= 1:
             begin(m - 1, 2)
-    for m in range(count):
-        for copy in flying[m]:
-            copy.wait_recv()
-        sent.extend(flying[m])
+        if m == 5:
+            begin(count - 1, 2)
+            for k in range(3):
+                arrive(k)
+            attend()
+    begin(count - 2, 2)
+    arrive(3)
+    stream1 = x_ref[...].astype(jnp.float32) + exchange(
+        0, dot_t(context_buf[...], weight(3)).astype(jnp.bfloat16)
+    )
+    normed2 = rms_scale(stream1, mlp_gain_ref[...]).astype(jnp.bfloat16)
+    arrive(4)
+    hidden = jnp.maximum(straight(normed2, 4), 0.0).astype(jnp.bfloat16)
+    arrive(5)
+    stream2 = stream1 + exchange(1, dot_t(hidden, weight(5)).astype(jnp.bfloat16))
+    stream2 = stream2.astype(jnp.bfloat16)
+    half = half_bf.shape[2]
+    half_bf[0] = stream2[:, :half]
+    half_bf[1] = stream2[:, half:]
+    arrive(6)
+    head_pre = straight(stream2, 6)
+    head_act = (head_pre / (1.0 + jnp.exp(-head_pre))).astype(jnp.bfloat16)
+    arrive(8)
+    skip = dot_t(half_bf[mp], weight(8))
+    arrive(7)
+    levels = dot_t(head_act, weight(7)) + skip
+    width = half_f32.shape[2]
+    for k in range(2):
+        part = levels[:, k * width : (k + 1) * width]
+        half_f32[k] = part
+        part_bf[k] = part.astype(jnp.bfloat16)
+    copy = pltpu.make_async_remote_copy(
+        src_ref=part_bf.at[1 - mp],
+        dst_ref=part_in,
+        send_sem=swap_send.at[2],
+        recv_sem=swap_recv.at[2],
+        device_id={"mp": 1 - mp},
+        device_id_type=MESH,
+    )
+    copy.start()
+    copy.wait()
+    out_ref[...] = half_f32[mp] + part_in[...].astype(jnp.float32)
     for copy in sent:
         copy.wait_send()
 
 
-def gather_all(owns, sizes):
-    rows, columns = owns[0].shape[1:]
-    counts = [own.shape[0] for own in owns]
-    count = sum(counts)
-    if rows % 16:
-        return lax.all_gather(jnp.concatenate(owns, axis=0), "dp", axis=1, tiled=True)
+def fused_block(sizes, *args):
+    x, keys, values, valid, attn_gain, mlp_gain, query_scale = args[:7]
+    w_qkv, w_out, w_up, w_down, head_hidden, final = args[7:]
+    rows, context_len, width = keys.shape
+    features = x.shape[1]
+    head_size = query_scale.shape[0]
+    lanes = 128
+    group = 16
+    valid_lanes = jnp.broadcast_to(valid.astype(jnp.bfloat16)[:, None], (rows, lanes))
+    spread = (jnp.arange(group * context_len)[:, None] // context_len == jnp.arange(group)).astype(
+        jnp.bfloat16
+    )
+    heads = (jnp.arange(lanes)[:, None] == jnp.arange(width) // head_size).astype(jnp.bfloat16)
+    scale = jnp.tile(query_scale, width // head_size)[None]
     slots = sum(size - 1 for size in sizes)
-    full = pl.pallas_call(
-        functools.partial(gather_kernel, sizes, axis_orders(count), counts),
-        out_shape=jax.ShapeDtypeStruct((count,) + sizes + (rows, columns), owns[0].dtype),
-        in_specs=[pl.BlockSpec(memory_space=pltpu.VMEM)] * len(owns),
-        out_specs=pl.BlockSpec(memory_space=pl.ANY),
+    own_rows = w_up.shape[0]
+    out_width = final.shape[2] * math.prod(sizes) // 2
+    vmem = pl.BlockSpec(memory_space=pltpu.VMEM)
+    hbm = pl.BlockSpec(memory_space=pl.ANY)
+    bf16, f32 = jnp.bfloat16, jnp.float32
+    return pl.pallas_call(
+        functools.partial(block_kernel, sizes, head_size),
+        out_shape=jax.ShapeDtypeStruct((rows, out_width), f32),
+        in_specs=[vmem, hbm, hbm] + [vmem] * 12,
+        out_specs=vmem,
         scratch_shapes=[
-            pltpu.SemaphoreType.DMA((count,)),
-            pltpu.SemaphoreType.DMA((count, slots)),
-            pltpu.SemaphoreType.DMA((count, slots)),
+            pltpu.VMEM((9,) + sizes + (own_rows, width), bf16),
+            pltpu.VMEM((rows * context_len, width), bf16),
+            pltpu.VMEM((rows * context_len, width), bf16),
+            pltpu.VMEM((rows, width), bf16),
+            pltpu.VMEM((2, rows, width), bf16),
+            pltpu.VMEM((rows, width), bf16),
+            pltpu.VMEM((2, rows, features), bf16),
+            pltpu.VMEM((2, rows, features), bf16),
+            pltpu.VMEM((2, rows, features // 2), bf16),
+            pltpu.VMEM((2, rows, out_width), f32),
+            pltpu.VMEM((2, rows, out_width), bf16),
+            pltpu.VMEM((rows, out_width), bf16),
+            pltpu.SemaphoreType.DMA((2,)),
+            pltpu.SemaphoreType.DMA((9,)),
+            pltpu.SemaphoreType.DMA((9, slots)),
+            pltpu.SemaphoreType.DMA((9, slots)),
+            pltpu.SemaphoreType.DMA((3,)),
+            pltpu.SemaphoreType.DMA((3,)),
         ],
-        compiler_params=pltpu.CompilerParams(collective_id=0, has_side_effects=True),
-        name="gather_weights",
-    )(*owns)
-    return full.reshape(count, math.prod(sizes) * rows, columns)
+        compiler_params=pltpu.CompilerParams(
+            collective_id=0, has_side_effects=True, vmem_limit_bytes=58 * 1024 * 1024
+        ),
+        name="decode_block",
+    )(
+        x,
+        keys.reshape(rows * context_len, width),
+        values.reshape(rows * context_len, width),
+        valid_lanes,
+        attn_gain[None],
+        mlp_gain[None],
+        scale,
+        spread,
+        heads,
+        w_qkv,
+        w_out.T,
+        w_up,
+        w_down.T,
+        head_hidden,
+        jnp.swapaxes(final, 1, 2),
+    )
+
+
+def gather_all(owns):
+    return lax.all_gather(jnp.concatenate(owns, axis=0), "dp", axis=1, tiled=True)
 
 
 def swap(values):
@@ -157,6 +363,23 @@
     head_hidden,
     final_layer_matrices,
 ):
+    if w_up.shape[0] % 16 == 0:
+        return fused_block(
+            sizes,
+            new_embed,
+            context_key_cache,
+            value_cache,
+            valid,
+            attn_gain,
+            mlp_gain,
+            query_scale,
+            w_qkv,
+            w_out,
+            w_up,
+            w_down,
+            head_hidden,
+            final_layer_matrices,
+        )
     row_count = new_embed.shape[0]
     context_len = context_key_cache.shape[1]
     local_width = context_key_cache.shape[2]
@@ -171,7 +394,7 @@
         head_hidden[None],
         jnp.swapaxes(final_layer_matrices, 1, 2),
     ]
-    full = gather_all(owns, sizes)
+    full = gather_all(owns)
     stream = new_embed.astype(jnp.float32)
     normed = rms_scale(stream, attn_gain).astype(jnp.bfloat16)
     projected = [jnp.dot(normed, full[j], preferred_element_type=jnp.float32) for j in range(3)]

time: 195 us -> 152 us (0.78); the launches traced: 193 us -> 152 us
  local copies, waits for them, and re-layouts: 20.9 us -> 6.28 us
  matrix products: 11.1 us -> 0 us
  Pallas kernels: 149 us -> 144 us
  starting transfers between devices: 4.02 us -> 0 us
  waiting for transfers between devices: 3.4 us -> 0 us
  other arithmetic: 4.21 us -> 2.1 us
    dot_general x7 -> x0, matrix products: 11.1 us -> none  [the longest x4 6.6 us: dot_t(): lax.dot_general(left, right, (((1,), (1,)), ((), ())), preferred_element_...]
    slice x1 -> x0, local copies, waits for them, and re-layouts: 9.94 us -> none  [per_device(): partial_out = dot_t(head_act, full[7]) + dot_t(stream_half, full[8])]
    unnamed x19 -> x1, local copies, waits for them, and re-layouts: 8.35 us -> 1.69 us
    pallas_call x1, Pallas kernels: 149 us -> 144 us  [fused_block(): pl.pallas_call(functools.partial(block_kernel, sizes, head_size), out_sha...]
    ppermute x3 -> x0, starting transfers between devices: 4.02 us -> none  [swap(): return lax.ppermute(values, 'mp', [(0, 1), (1, 0)])]
    ppermute x3 -> x0, waiting for transfers between devices: 3.4 us -> none  [swap(): return lax.ppermute(values, 'mp', [(0, 1), (1, 0)])]
    broadcast_in_dim x0 -> x3, local copies, waits for them, and re-layouts: none -> 3.26 us  [the longest x1 1.29 us: fused_block(): mlp_gain[None]]
    dot_general x1 -> x0, local copies, waits for them, and re-layouts: 2.21 us -> none  [per_device(): jnp.dot(normed, full[j], preferred_element_type=jnp.float32)]
  transfers between devices with their start and end apart: 3 -> 0, of which waited for: 3 -> 0; matrix products, arithmetic and copies ran while one was open for 0% -> 0% of each run, Pallas kernels for 0% -> 0%
where the time goes in v3:
time: 152 us
  Pallas kernels  144 us (95%)
  local copies, waits for them, and re-layouts  6.28 us (4%)
  other arithmetic  2.1 us (1%)
    pallas_call x1, Pallas kernels, fused_block(): pl.pallas_call(functools.partial(block_kernel, sizes, head_size), out_sha...  144 us

profile of v3, /device:TPU:13, one launch (start us, length us, event | category | flops | bytes accessed | tf_op | source)
XLA Modules:
  0.0 152.1 jit_solution(6962394361443614683)
XLA Ops:
  0.0 0.7 convert_element_type.9
  0.7 0.7 tile.2
  1.3 0.7 broadcast_in_dim_tile.3.scale_ref
  2.0 1.3 broadcast_in_dim.7.attn_gain_ref
  3.3 1.3 broadcast_in_dim.8.mlp_gain_ref
  4.6 0.7 broadcast_in_dim.6.valid_ref
  5.3 0.7 fusion.1.spread_ref
  6.0 0.7 fusion.heads_ref
  6.7 143.7 %decode_block.1 = f32[112,640]{1,0:T(8,128)} custom-call(bf16[112,1280]{1,0:T(8,128)(2,1)} %x_ref.1, bf16[1792,640]{1,0:T(8,128)(2,1)} %bitcast.5, bf16[1792,640]{1,0:T(8,128)(2,1)} %bitcast.6, bf16[112,128]{1,0:T(8,128)(2,1)} %broadcast_in_dim.6.valid_ref, f32[1,1280]{1,0:T(1,128)} %broadcast_in_dim.7.attn_gain_ref, ...), custom_call_target="tpu_custom_call" | custom-call | tf_op jit(solution)/shard_map/decode_block/pallas_call | solution.py:283
  150.4 1.7 %copy.15 = f32[112,640]{1,0:T(8,128)} copy(f32[112,640]{1,0:T(8,128)} %decode_block.1) | data formatting | bytes 573440
  (2 shorter events, 0.0 us)

commit v4 on v3

--- a/solution.py
+++ b/solution.py
@@ -24,8 +24,8 @@
 
 
 def axis_orders(count):
-    pair = ((0, 1, 2), (0, 2, 1))
-    return [pair[m % 2] for m in range(count - 1)] + [(2, 1, 0)]
+    pattern = ((0, 1, 2), (0, 2, 1), (0, 1, 2), (0, 2, 1), (0, 1, 2), (0, 2, 1), (0, 1, 2), (2, 1, 0), (1, 2, 0))
+    return [pattern[m % len(pattern)] for m in range(count)]
 
 
 def block_kernel(
@@ -123,7 +123,8 @@
             copy.start()
 
     ahead = 3
-    for m in [0, count - 1] + list(range(1, ahead)):
+    plain = count - 2
+    for m in [0] + list(range(plain, count)) + list(range(1, ahead)):
         begin(m, 0)
     local = []
     for m in range(count):
@@ -134,7 +135,8 @@
         copy.start()
     for copy in local:
         copy.wait()
-    begin(count - 1, 1)
+    for m in range(plain, count):
+        begin(m, 1)
 
     def weight(m):
         held = full_ref[m]
@@ -208,18 +210,20 @@
 
         lax.fori_loop(0, query_buf.shape[0] // rows, chunk, 0)
 
-    for m in range(count - 1):
+    for m in range(plain):
         begin(m, 1)
-        if m + ahead < count - 1:
+        if m + ahead < plain:
             begin(m + ahead, 0)
         if m >= 1:
             begin(m - 1, 2)
+        if m == 3:
+            for k in range(plain, count):
+                begin(k, 2)
         if m == 5:
-            begin(count - 1, 2)
             for k in range(3):
                 arrive(k)
             attend()
-    begin(count - 2, 2)
+    begin(plain - 1, 2)
     arrive(3)
     stream1 = x_ref[...].astype(jnp.float32) + exchange(
         0, dot_t(context_buf[...], weight(3)).astype(jnp.bfloat16)

time: 152 us -> 150 us (0.987)
  Pallas kernels: 144 us -> 141 us
    pallas_call x1, Pallas kernels: 144 us -> 141 us  [fused_block(): pl.pallas_call(functools.partial(block_kernel, sizes, head_size), out_sha...]
where the time goes in v4:
time: 150 us
  Pallas kernels  141 us (94%)
  local copies, waits for them, and re-layouts  6.28 us (4%)
  other arithmetic  2.1 us (1%)
    pallas_call x1, Pallas kernels, fused_block(): pl.pallas_call(functools.partial(block_kernel, sizes, head_size), out_sha...  141 us

profile of v4, /device:TPU:13, one launch (start us, length us, event | category | flops | bytes accessed | tf_op | source)
XLA Modules:
  0.0 149.6 jit_solution(16185432187014831155)
XLA Ops:
  0.0 0.7 convert_element_type.9
  0.7 0.7 tile.2
  1.3 0.7 broadcast_in_dim_tile.3.scale_ref
  2.0 1.3 broadcast_in_dim.7.attn_gain_ref
  3.3 1.3 broadcast_in_dim.8.mlp_gain_ref
  4.6 0.7 broadcast_in_dim.6.valid_ref
  5.3 0.7 fusion.1.spread_ref
  6.0 0.7 fusion.heads_ref
  6.7 141.2 %decode_block.1 = f32[112,640]{1,0:T(8,128)} custom-call(bf16[112,1280]{1,0:T(8,128)(2,1)} %x_ref.1, bf16[1792,640]{1,0:T(8,128)(2,1)} %bitcast.5, bf16[1792,640]{1,0:T(8,128)(2,1)} %bitcast.6, bf16[112,128]{1,0:T(8,128)(2,1)} %broadcast_in_dim.6.valid_ref, f32[1,1280]{1,0:T(1,128)} %broadcast_in_dim.7.attn_gain_ref, ...), custom_call_target="tpu_custom_call" | custom-call | tf_op jit(solution)/shard_map/decode_block/pallas_call | solution.py:287
  147.9 1.7 %copy.15 = f32[112,640]{1,0:T(8,128)} copy(f32[112,640]{1,0:T(8,128)} %decode_block.1) | data formatting | bytes 573440
  (2 shorter events, 0.0 us)
